TPU v7x, 256 devices: a whole 4x4x8 slice. The times are simulated.
256 devices in a mesh: blk: 128 (over z, y_lo, x, core), dp: 2 (over y_hi).
Axes of the slice: x: 4, y: 4 (y_hi: 2, y_lo: 2; y = y_hi * 2 + y_lo), z: 8, core: 2. Of those that a mesh axis runs over, the one named last changes fastest.
Arguments:
- tokens: bfloat16 [49152, 2048], P(('blk', 'dp')), may hold values from -6 to 6
- cotangent: bfloat16 [49152, 2048], P(('blk', 'dp')), may hold values from -0.59765625 to 0.59765625
- gate_probs: bfloat16 [49152, 3], P(('blk', 'dp')), may hold values from 0.099609375 to 1
- slot_rows: int32 [384, 128], P('blk'), may hold values from 0 to 384, as said below
- w_gate: bfloat16 [128, 2048, 768], P('blk', None, 'dp'), may hold values from -0.125 to 0.125
- w_up: bfloat16 [128, 2048, 768], P('blk', None, 'dp'), may hold values from -0.125 to 0.125
- w_down: bfloat16 [128, 768, 2048], P('blk', 'dp'), may hold values from -0.21875 to 0.21875
Outputs:
- mixed: bfloat16 [49152, 2048], P(('blk', 'dp'))
- input_grad: bfloat16 [49152, 2048], P(('blk', 'dp'))
- gate_grad: float32 [49152, 3], P(('blk', 'dp'))
- w_gate_grad: bfloat16 [128, 2048, 768], P('blk', None, 'dp')
- w_up_grad: bfloat16 [128, 2048, 768], P('blk', None, 'dp')
- w_down_grad: bfloat16 [128, 768, 2048], P('blk', 'dp')
Inputs may be any that keep to these rules, and one draw needn't show every extreme that they name: `slot_rows`: entries below 384 in a row are distinct and stand before the entries equal to 384; every row names at least 16 tokens, and some row names 128.
All inputs are finite; a program needn't handle non-finite values.
Results may differ from a plain program's by a relative error of at most 0.0075.
Values may be sent and summed in bfloat16 or wider, within the bound.
A program may use at most 128 MiB of HBM per device.

v0:
```python
import jax
import jax.numpy as jnp
from jax import lax
from jax.sharding import PartitionSpec as P

BF = jnp.bfloat16
F32 = jnp.float32


def shifted(value, axis, steps):
    count = lax.axis_size(axis)
    pairs = [(source, (source + steps) % count) for source in range(count)]
    return lax.ppermute(value, axis, pairs)


def on_device(tokens, cotangent, gate_probs, slot_rows, w_gate, w_up, w_down):
    half = lax.axis_index("dp")
    own = tokens.shape[0]
    group_x = lax.all_gather(tokens, "dp", axis=0, tiled=True)
    group_dy = lax.all_gather(cotangent, "dp", axis=0, tiled=True)
    group_gate = lax.all_gather(gate_probs, "dp", axis=0, tiled=True)
    cycle, cap = slot_rows.shape
    group = group_x.shape[0]
    names = slot_rows[:, :, None] == lax.broadcasted_iota(jnp.int32, (1, 1, group), 2)
    picks = names.astype(BF)
    rows_x = jnp.einsum("sct,td->scd", picks, group_x, preferred_element_type=F32).astype(BF)
    rows_dy = jnp.einsum("sct,td->scd", picks, group_dy, preferred_element_type=F32).astype(BF)
    rows_gate = jnp.einsum("sct,ts->sc", picks, group_gate, preferred_element_type=F32).astype(BF)
    lists_x, lists_dy, lists_gate = ([rows_x[0]], [rows_dy[0]], [rows_gate[0]])
    for step in range(1, cycle):
        lists_x.append(shifted(rows_x[step], "blk", -step))
        lists_dy.append(shifted(rows_dy[step], "blk", -step))
        lists_gate.append(shifted(rows_gate[step], "blk", -step))
    x = jnp.concatenate(lists_x, axis=0)
    dy = jnp.concatenate(lists_dy, axis=0)
    gate = jnp.concatenate(lists_gate, axis=0).astype(F32)[:, None]
    w_g, w_u, w_d = (w_gate[0], w_up[0], w_down[0])
    pre_gate = jnp.dot(x, w_g, preferred_element_type=F32)
    pre_up = jnp.dot(x, w_u, preferred_element_type=F32)
    back = jnp.einsum("cd,hd->ch", dy, w_d, preferred_element_type=F32)
    sig = jax.nn.sigmoid(pre_gate)
    active = pre_gate * sig
    hidden = active * pre_up
    gate_part = jnp.sum(hidden * back, axis=1)
    hidden_w = (hidden * gate).astype(BF)
    hidden_grad = back * gate
    pgg = (hidden_grad * pre_up * sig * (1.0 + pre_gate * (1.0 - sig))).astype(BF)
    pug = (hidden_grad * active).astype(BF)
    weighted = jnp.dot(hidden_w, w_d, preferred_element_type=F32).astype(BF)
    in_grad = jnp.einsum("ch,dh->cd", pgg, w_g, preferred_element_type=F32)
    in_grad = in_grad + jnp.einsum("ch,dh->cd", pug, w_u, preferred_element_type=F32)
    in_grad = in_grad.astype(BF)
    out_w, out_i, out_g = ([weighted[:cap]], [in_grad[:cap]], [gate_part[:cap]])
    for step in range(1, cycle):
        rows = slice(step * cap, (step + 1) * cap)
        out_w.append(shifted(weighted[rows], "blk", step))
        out_i.append(shifted(in_grad[rows], "blk", step))
        out_g.append(shifted(gate_part[rows], "blk", step))
    d_gate = jnp.einsum("cd,ch->dh", x, pgg, preferred_element_type=F32).astype(BF)
    d_up = jnp.einsum("cd,ch->dh", x, pug, preferred_element_type=F32).astype(BF)
    d_down = jnp.einsum("ch,cd->hd", hidden_w, dy, preferred_element_type=F32).astype(BF)
    back_w = jnp.concatenate(out_w, axis=0)
    back_i = jnp.concatenate(out_i, axis=0)
    flat = picks.reshape(cycle * cap, group)
    mixed = jnp.einsum("ct,cd->td", flat, back_w, preferred_element_type=F32)
    input_grad = jnp.einsum("ct,cd->td", flat, back_i, preferred_element_type=F32)
    gate_grad = jnp.stack(
        [jnp.sum(jnp.where(names[s], out_g[s][:, None], 0.0), axis=0) for s in range(cycle)], axis=1
    )

    def summed(full, kind):
        mine = lax.dynamic_slice_in_dim(full, half * own, own, 0)
        other = lax.dynamic_slice_in_dim(full, (1 - half) * own, own, 0)
        arrived = lax.ppermute(other.astype(kind), "dp", [(0, 1), (1, 0)])
        return mine + arrived.astype(F32)

    return (
        summed(mixed, BF).astype(BF),
        summed(input_grad, BF).astype(BF),
        summed(gate_grad, F32),
        d_gate[None],
        d_up[None],
        d_down[None],
    )


def solution(mesh):
    in_specs = (
        P(("blk", "dp"), None),
        P(("blk", "dp"), None),
        P(("blk", "dp"), None),
        P("blk", None),
        P("blk", None, "dp"),
        P("blk", None, "dp"),
        P("blk", "dp", None),
    )
    out_specs = (
        P(("blk", "dp"), None),
        P(("blk", "dp"), None),
        P(("blk", "dp"), None),
        P("blk", None, "dp"),
        P("blk", None, "dp"),
        P("blk", "dp", None),
    )
    return jax.shard_map(
        on_device, mesh=mesh, in_specs=in_specs, out_specs=out_specs, check_vma=False
    )
```

profile of v0, /device:TPU:1, one launch (start us, length us, event | category | flops | bytes accessed | tf_op | source)
XLA Modules:
  0.0 200.9 jit_solution(9624781532558431168)
XLA Ops:
  7.2 0.7 all-gather.4.cloned.1.call-update
  8.0 0.7 all-gather.6.cloned.1.call-update
  8.7 5.5 %all-gather = bf16[2,192,3]{1,2,0:T(4,128)(2,1)S(1)} all-gather(bf16[1,192,3]{1,2,0:T(4,128)(2,1)S(1)} %bitcast.76), channel_id=1, replica_groups=mesh['blk'=128,'dp'=2] {'dp'}, dimensions={0}, use_global_device_ids=true | all-gather | bytes 3456 | tf_op jit(solution)/shard_map/all_gather | solution.py:21
  14.3 0.3 fusion.28
  14.6 8.9 %collective-permute-start.3 = (bf16[128]{0:T(256)(128)(2,1)S(1)}, bf16[128]{0:T(256)(128)(2,1)S(1)}, u32[]{:S(2)}, u32[]{:S(2)}) collective-permute-start(bf16[128]{0:T(256)(128)(2,1)S(1)} %get-tuple-element.29), channel_id=1, source_target_pairs={{0,252},{2,254},{4,0},{6,2},{8,4},{10,6},{12,8},{14,10},{16,12},{1... | collective-permute-start | bytes 776 | tf_op jit(solution)/shard_map/ppermute | solution.py:13
  23.5 2.1 %collective-permute-start.2 = (bf16[128]{0:T(256)(128)(2,1)S(1)}, bf16[128]{0:T(256)(128)(2,1)S(1)}, u32[]{:S(2)}, u32[]{:S(2)}) collective-permute-start(bf16[128]{0:T(256)(128)(2,1)S(1)} %get-tuple-element.30), channel_id=1, source_target_pairs={{0,254},{2,0},{4,2},{6,4},{8,6},{10,8},{12,10},{14,12},{16,14},{18... | collective-permute-start | bytes 776 | tf_op jit(solution)/shard_map/ppermute | solution.py:13
  25.6 0.1 iota_compare_fusion
  25.8 0.7 collective-permute-done.2
  26.5 20.7 %all-gather.4.cloned.1.call-done = bf16[384,2048]{1,0:T(8,128)(2,1)} async-done(((bf16[192,2048]{1,0:T(8,128)(2,1)}), bf16[384,2048]{1,0:T(8,128)(2,1)}) %all-gather.4.cloned.1.call-update) | async-done | bytes 1572880 | tf_op jit(solution)/shard_map/all_gather | solution.py:19
  47.3 2.4 %convolution_convert_fusion.5 = bf16[3,128,2048]{2,1,0:T(8,128)(2,1)S(1)} fusion(bf16[384,2048]{1,0:T(8,128)(2,1)} %all-gather.4.cloned.1.call-done, s32[3,128]{1,0:T(4,128)S(1)} %copy-done.3), kind=kOutput, calls=%fused_computation.6 | convolution fusion | flops 604913664 | bytes 3147264 | tf_op jit(solution)/shard_map/sct,td->scd/dot_general | solution.py:26
  49.7 0.2 slice_bitcast_fusion.5
  49.9 5.3 %collective-permute-start.1 = (bf16[128,2048]{1,0:T(8,128)(2,1)S(1)}, bf16[128,2048]{1,0:T(8,128)(2,1)}, u32[]{:S(2)}, u32[]{:S(2)}) collective-permute-start(bf16[128,2048]{1,0:T(8,128)(2,1)S(1)} %get-tuple-element.21), channel_id=1, source_target_pairs={{0,252},{2,254},{4,0},{6,2},{8,4},{10,6},{12,8},{14,10},{16,12},{1... | collective-permute-start | bytes 1572872 | tf_op jit(solution)/shard_map/ppermute | solution.py:13
  55.1 1.1 collective-permute-start
  56.3 26.1 %all-gather.6.cloned.1.call-done = bf16[384,2048]{1,0:T(8,128)(2,1)} async-done(((bf16[192,2048]{1,0:T(8,128)(2,1)}), bf16[384,2048]{1,0:T(8,128)(2,1)}) %all-gather.6.cloned.1.call-update) | async-done | bytes 1572880 | tf_op jit(solution)/shard_map/all_gather | solution.py:20
  82.3 2.4 %convolution_convert_fusion.3 = bf16[3,128,2048]{2,1,0:T(8,128)(2,1)S(1)} fusion(bf16[384,2048]{1,0:T(8,128)(2,1)} %all-gather.6.cloned.1.call-done, s32[3,128]{1,0:T(4,128)S(1)} %copy-done.3), kind=kOutput, calls=%fused_computation.4 | convolution fusion | flops 604913664 | bytes 3147264 | tf_op jit(solution)/shard_map/sct,td->scd/dot_general | solution.py:27
  84.9 10.9 %collective-permute-start.8 = (bf16[128,2048]{1,0:T(8,128)(2,1)S(1)}, bf16[128,2048]{1,0:T(8,128)(2,1)S(1)}, u32[]{:S(2)}, u32[]{:S(2)}) collective-permute-start(bf16[128,2048]{1,0:T(8,128)(2,1)S(1)} %get-tuple-element.15), channel_id=1, source_target_pairs={{0,252},{2,254},{4,0},{6,2},{8,4},{10,6},{12,8},{14,10},{16,12},{1... | collective-permute-start | bytes 1572872 | tf_op jit(solution)/shard_map/ppermute | solution.py:13
  95.8 0.8 collective-permute-start.7
  96.6 2.4 %fusion.20 = f32[384,384]{0,1:T(8,128)S(1)} fusion(bf16[1,2048,384]{2,1,0:T(8,128)(2,1)S(1)} %copy-done.2, bf16[128,2048]{1,0:T(8,128)(2,1)} %collective-permute-done.1, bf16[128,2048]{1,0:T(8,128)(2,1)} %collective-permute-done, bf16[128,2048]{1,0:T(8,128)(2,1)S(1)} %get-tuple-element.20), kind=kOutput, calls=%fused_computation.29 | convolution fusion | flops 608698368 | bytes 3735552 | tf_op jit(solution)/shard_map/dot_general | solution.py:39
  98.9 2.2 %fusion.24 = f32[384,384]{0,1:T(8,128)S(1)} fusion(bf16[1,2048,384]{2,1,0:T(8,128)(2,1)S(1)} %copy-done.1, bf16[128,2048]{1,0:T(8,128)(2,1)} %collective-permute-done.1, bf16[128,2048]{1,0:T(8,128)(2,1)} %collective-permute-done, bf16[128,2048]{1,0:T(8,128)(2,1)S(1)} %get-tuple-element.20), kind=kOutput, calls=%fused_computation.33 | convolution fusion | flops 608698368 | bytes 3735552 | tf_op jit(solution)/shard_map/dot_general | solution.py:38
  101.2 5.3 %collective-permute-done.8 = bf16[128,2048]{1,0:T(8,128)(2,1)S(1)} collective-permute-done((bf16[128,2048]{1,0:T(8,128)(2,1)S(1)}, bf16[128,2048]{1,0:T(8,128)(2,1)S(1)}, u32[]{:S(2)}, u32[]{:S(2)}) %collective-permute-start.8) | collective-permute-done | bytes 524320 | tf_op jit(solution)/shard_map/ppermute | solution.py:13
  106.5 1.2 multiply_reduce_fusion
  107.8 1.0 convolution_convert_fusion.4
  108.8 0.1 fusion.39
  109.0 2.5 %collective-permute-start.4 = (bf16[128,2048]{1,0:T(8,128)(2,1)S(1)}, bf16[128,2048]{1,0:T(8,128)(2,1)S(1)}, u32[]{:S(2)}, u32[]{:S(2)}) collective-permute-start(bf16[128,2048]{1,0:T(8,128)(2,1)S(1)} %get-tuple-element.19), channel_id=1, source_target_pairs={{0,2},{2,4},{4,6},{6,8},{8,10},{10,12},{12,14},{14,16},{16,18},{18... | collective-permute-start | bytes 1572872 | tf_op jit(solution)/shard_map/ppermute | solution.py:13
  111.5 1.0 fusion.22
  112.5 1.0 add_convert_fusion
  113.6 0.2 fusion.38
  113.7 5.0 %collective-permute-start.10 = (bf16[128,2048]{1,0:T(8,128)(2,1)S(1)}, bf16[128,2048]{1,0:T(8,128)(2,1)S(1)}, u32[]{:S(2)}, u32[]{:S(2)}) collective-permute-start(bf16[128,2048]{1,0:T(8,128)(2,1)S(1)} %get-tuple-element.12), channel_id=1, source_target_pairs={{0,4},{2,6},{4,8},{6,10},{8,12},{10,14},{12,16},{14,18},{16,20},{1... | collective-permute-start | bytes 1572872 | tf_op jit(solution)/shard_map/ppermute | solution.py:13
  118.7 3.6 %collective-permute-start.13 = (f32[128]{0:T(128)S(1)}, f32[128]{0:T(128)S(1)}, u32[]{:S(2)}, u32[]{:S(2)}) collective-permute-start(f32[128]{0:T(128)S(1)} %get-tuple-element.26), channel_id=1, source_target_pairs={{0,4},{2,6},{4,8},{6,10},{8,12},{10,14},{12,16},{14,18},{16,20},{1... | collective-permute-start | bytes 1544 | tf_op jit(solution)/shard_map/ppermute | solution.py:13
  122.3 1.1 collective-permute-start.12
  123.4 3.5 %fusion = bf16[1,2048,384]{2,1,0:T(8,128)(2,1)} fusion(bf16[384,384]{0,1:T(8,128)(2,1)S(1)} %get-tuple-element.10, bf16[128,2048]{1,0:T(8,128)(2,1)} %collective-permute-done.1, bf16[128,2048]{1,0:T(8,128)(2,1)} %collective-permute-done, bf16[128,2048]{1,0:T(8,128)(2,1)S(1)} %get-tuple-element.20), kind=kOutput, calls=%fused_computation.7 | convolution fusion | flops 609484800 | bytes 3440640 | tf_op jit(solution)/shard_map/cd,ch->dh/dot_general | solution.py:59
  126.9 3.5 %fusion.1 = bf16[1,2048,384]{2,1,0:T(8,128)(2,1)} fusion(bf16[384,384]{0,1:T(8,128)(2,1)S(1)} %get-tuple-element.24, bf16[128,2048]{1,0:T(8,128)(2,1)} %collective-permute-done.1, bf16[128,2048]{1,0:T(8,128)(2,1)} %collective-permute-done, bf16[128,2048]{1,0:T(8,128)(2,1)S(1)} %get-tuple-element.20), kind=kOutput, calls=%fused_computation.8 | convolution fusion | flops 609484800 | bytes 3440640 | tf_op jit(solution)/shard_map/cd,ch->dh/dot_general | solution.py:60
  130.5 20.4 %collective-permute-done.13 = f32[128]{0:T(128)S(1)} collective-permute-done((f32[128]{0:T(128)S(1)}, f32[128]{0:T(128)S(1)}, u32[]{:S(2)}, u32[]{:S(2)}) %collective-permute-start.13) | collective-permute-done | bytes 544 | tf_op jit(solution)/shard_map/ppermute | solution.py:13
  150.8 0.2 select_reduce_fusion.2
  151.1 4.0 %collective-permute-start.14 = (f32[192,3]{0,1:T(4,128)S(1)}, f32[192,3]{0,1:T(4,128)S(1)}, u32[]{:S(2)}, u32[]{:S(2)}) collective-permute-start(f32[192,3]{0,1:T(4,128)S(1)} %constant_dynamic-slice_fusion), channel_id=1, source_target_pairs={{0,1},{1,0},{2,3},{3,2},{4,5},{5,4},{6,7},{7,6},{8,9},{9,8},{10,11... | collective-permute-start | bytes 6920 | tf_op jit(solution)/shard_map/ppermute | solution.py:74
  155.1 1.1 fusion.3
  156.2 0.1 dynamic-slice_convert_fusion.1
  156.4 0.1 collective-permute-start.6
  156.5 0.5 collective-permute-done.9
  156.9 1.1 fusion.9
  158.0 0.1 dynamic-slice_convert_fusion
  158.2 4.1 %collective-permute-start.11 = (bf16[192,2048]{1,0:T(8,128)(2,1)S(1)}, bf16[192,2048]{1,0:T(8,128)(2,1)S(1)}, u32[]{:S(2)}, u32[]{:S(2)}) collective-permute-start(bf16[192,2048]{1,0:T(8,128)(2,1)S(1)} %dynamic-slice_convert_fusion), channel_id=1, source_target_pairs={{0,1},{1,0},{2,3},{3,2},{4,5},{5,4},{6,7},{7,6},{8,9},{9,8},{10,11... | collective-permute-start | bytes 2359304 | tf_op jit(solution)/shard_map/ppermute | solution.py:74
  162.2 2.1 %fusion.2 = bf16[1,384,2048]{2,1,0:T(8,128)(2,1)} fusion(bf16[384,384]{0,1:T(8,128)(2,1)S(1)} %get-tuple-element.23, bf16[128,2048]{1,0:T(8,128)(2,1)S(1)} %collective-permute-done.8, bf16[128,2048]{1,0:T(8,128)(2,1)S(1)} %collective-permute-done.7, bf16[128,2048]{1,0:T(8,128)(2,1)S(1)} %get-tuple-element.14), kind=kOutput, calls=%fused_computation.9 | convolution fusion | flops 609484800 | bytes 3440640 | tf_op jit(solution)/shard_map/ch,cd->hd/dot_general | solution.py:61
  164.4 0.7 dynamic-slice_add_fusion
  165.0 11.1 %collective-permute-done.6 = bf16[192,2048]{1,0:T(8,128)(2,1)S(1)} collective-permute-done((bf16[192,2048]{1,0:T(8,128)(2,1)S(1)}, bf16[192,2048]{1,0:T(8,128)(2,1)S(1)}, u32[]{:S(2)}, u32[]{:S(2)}) %collective-permute-start.6) | collective-permute-done | bytes 786464 | tf_op jit(solution)/shard_map/ppermute | solution.py:74
  176.2 1.1 add_convert_fusion.2
  177.2 15.8 %collective-permute-done.11 = bf16[192,2048]{1,0:T(8,128)(2,1)S(1)} collective-permute-done((bf16[192,2048]{1,0:T(8,128)(2,1)S(1)}, bf16[192,2048]{1,0:T(8,128)(2,1)S(1)}, u32[]{:S(2)}, u32[]{:S(2)}) %collective-permute-start.11) | collective-permute-done | bytes 786464 | tf_op jit(solution)/shard_map/ppermute | solution.py:74
  193.0 1.1 add_convert_fusion.1
  (35 shorter events, 0.6 us)
Async XLA Ops:
  7.2 99.4 %copy-start = (bf16[1,384,2048]{2,1,0:T(8,128)(2,1)S(1)}, bf16[1,384,2048]{2,1,0:T(8,128)(2,1)}, u32[]{:S(2)}) copy-start(bf16[1,384,2048]{2,1,0:T(8,128)(2,1)} %param.13) | copy-start | bytes 4718596
  7.2 1.5 copy-start.4
  7.2 7.1 %copy-start.3 = (s32[3,128]{1,0:T(4,128)S(1)}, s32[3,128]{1,0:T(4,128)}, u32[]{:S(2)}) copy-start(s32[3,128]{1,0:T(4,128)} %param.10) | copy-start | bytes 4612
  7.2 40.1 %all-gather.4.cloned.1.call-start = ((), (), s32[]{:S(2)}) async-start(), calls=%async_computation | async-start | bytes 2359296 | tf_op jit(solution)/shard_map/all_gather | solution.py:19
  7.9 74.4 %all-gather.6.cloned.1.call-start = ((), (), s32[]{:S(2)}) async-start(), calls=%async_computation.1 | async-start | bytes 2359296 | tf_op jit(solution)/shard_map/all_gather | solution.py:20
  14.6 11.2 %collective-permute-start.3 = (bf16[128]{0:T(256)(128)(2,1)S(1)}, bf16[128]{0:T(256)(128)(2,1)S(1)}, u32[]{:S(2)}, u32[]{:S(2)}) collective-permute-start(bf16[128]{0:T(256)(128)(2,1)S(1)} %get-tuple-element.29), channel_id=1, source_target_pairs={{0,252},{2,254},{4,0},{6,2},{8,4},{10,6},{12,8},{14,10},{16,12},{1... | collective-permute-start | bytes 776 | tf_op jit(solution)/shard_map/ppermute | solution.py:13
  23.5 3.0 %collective-permute-start.2 = (bf16[128]{0:T(256)(128)(2,1)S(1)}, bf16[128]{0:T(256)(128)(2,1)S(1)}, u32[]{:S(2)}, u32[]{:S(2)}) collective-permute-start(bf16[128]{0:T(256)(128)(2,1)S(1)} %get-tuple-element.30), channel_id=1, source_target_pairs={{0,254},{2,0},{4,2},{6,4},{8,6},{10,8},{12,10},{14,12},{16,14},{18... | collective-permute-start | bytes 776 | tf_op jit(solution)/shard_map/ppermute | solution.py:13
  49.9 46.7 %collective-permute-start.1 = (bf16[128,2048]{1,0:T(8,128)(2,1)S(1)}, bf16[128,2048]{1,0:T(8,128)(2,1)}, u32[]{:S(2)}, u32[]{:S(2)}) collective-permute-start(bf16[128,2048]{1,0:T(8,128)(2,1)S(1)} %get-tuple-element.21), channel_id=1, source_target_pairs={{0,252},{2,254},{4,0},{6,2},{8,4},{10,6},{12,8},{14,10},{16,12},{1... | collective-permute-start | bytes 1572872 | tf_op jit(solution)/shard_map/ppermute | solution.py:13
  55.1 41.4 %collective-permute-start = (bf16[128,2048]{1,0:T(8,128)(2,1)S(1)}, bf16[128,2048]{1,0:T(8,128)(2,1)}, u32[]{:S(2)}, u32[]{:S(2)}) collective-permute-start(bf16[128,2048]{1,0:T(8,128)(2,1)S(1)} %get-tuple-element.22), channel_id=1, source_target_pairs={{0,254},{2,0},{4,2},{6,4},{8,6},{10,8},{12,10},{14,12},{16,14},{18... | collective-permute-start | bytes 1572872 | tf_op jit(solution)/shard_map/ppermute | solution.py:13
  84.8 11.8 %copy-start.2 = (bf16[1,2048,384]{2,1,0:T(8,128)(2,1)S(1)}, bf16[1,2048,384]{2,1,0:T(8,128)(2,1)}, u32[]{:S(2)}) copy-start(bf16[1,2048,384]{2,1,0:T(8,128)(2,1)} %param.12) | copy-start | bytes 4718596
  84.9 21.7 %collective-permute-start.8 = (bf16[128,2048]{1,0:T(8,128)(2,1)S(1)}, bf16[128,2048]{1,0:T(8,128)(2,1)S(1)}, u32[]{:S(2)}, u32[]{:S(2)}) collective-permute-start(bf16[128,2048]{1,0:T(8,128)(2,1)S(1)} %get-tuple-element.15), channel_id=1, source_target_pairs={{0,252},{2,254},{4,0},{6,2},{8,4},{10,6},{12,8},{14,10},{16,12},{1... | collective-permute-start | bytes 1572872 | tf_op jit(solution)/shard_map/ppermute | solution.py:13
  95.8 10.8 %collective-permute-start.7 = (bf16[128,2048]{1,0:T(8,128)(2,1)S(1)}, bf16[128,2048]{1,0:T(8,128)(2,1)S(1)}, u32[]{:S(2)}, u32[]{:S(2)}) collective-permute-start(bf16[128,2048]{1,0:T(8,128)(2,1)S(1)} %get-tuple-element.16), channel_id=1, source_target_pairs={{0,254},{2,0},{4,2},{6,4},{8,6},{10,8},{12,10},{14,12},{16,14},{18... | collective-permute-start | bytes 1572872 | tf_op jit(solution)/shard_map/ppermute | solution.py:13
  96.6 2.4 %copy-start.1 = (bf16[1,2048,384]{2,1,0:T(8,128)(2,1)S(1)}, bf16[1,2048,384]{2,1,0:T(8,128)(2,1)}, u32[]{:S(2)}) copy-start(bf16[1,2048,384]{2,1,0:T(8,128)(2,1)} %param.11) | copy-start | bytes 4718596
  108.9 46.2 %collective-permute-start.5 = (bf16[128,2048]{1,0:T(8,128)(2,1)S(1)}, bf16[128,2048]{1,0:T(8,128)(2,1)S(1)}, u32[]{:S(2)}, u32[]{:S(2)}) collective-permute-start(bf16[128,2048]{1,0:T(8,128)(2,1)S(1)} %get-tuple-element.18), channel_id=1, source_target_pairs={{0,4},{2,6},{4,8},{6,10},{8,12},{10,14},{12,16},{14,18},{16,20},{1... | collective-permute-start | bytes 1572872 | tf_op jit(solution)/shard_map/ppermute | solution.py:13
  109.0 46.1 %collective-permute-start.4 = (bf16[128,2048]{1,0:T(8,128)(2,1)S(1)}, bf16[128,2048]{1,0:T(8,128)(2,1)S(1)}, u32[]{:S(2)}, u32[]{:S(2)}) collective-permute-start(bf16[128,2048]{1,0:T(8,128)(2,1)S(1)} %get-tuple-element.19), channel_id=1, source_target_pairs={{0,2},{2,4},{4,6},{6,8},{8,10},{10,12},{12,14},{14,16},{16,18},{18... | collective-permute-start | bytes 1572872 | tf_op jit(solution)/shard_map/ppermute | solution.py:13
  113.7 42.7 %collective-permute-start.10 = (bf16[128,2048]{1,0:T(8,128)(2,1)S(1)}, bf16[128,2048]{1,0:T(8,128)(2,1)S(1)}, u32[]{:S(2)}, u32[]{:S(2)}) collective-permute-start(bf16[128,2048]{1,0:T(8,128)(2,1)S(1)} %get-tuple-element.12), channel_id=1, source_target_pairs={{0,4},{2,6},{4,8},{6,10},{8,12},{10,14},{12,16},{14,18},{16,20},{1... | collective-permute-start | bytes 1572872 | tf_op jit(solution)/shard_map/ppermute | solution.py:13
  118.7 32.1 %collective-permute-start.13 = (f32[128]{0:T(128)S(1)}, f32[128]{0:T(128)S(1)}, u32[]{:S(2)}, u32[]{:S(2)}) collective-permute-start(f32[128]{0:T(128)S(1)} %get-tuple-element.26), channel_id=1, source_target_pairs={{0,4},{2,6},{4,8},{6,10},{8,12},{10,14},{12,16},{14,18},{16,20},{1... | collective-permute-start | bytes 1544 | tf_op jit(solution)/shard_map/ppermute | solution.py:13
  122.3 28.5 %collective-permute-start.12 = (f32[128]{0:T(128)S(1)}, f32[128]{0:T(128)S(1)}, u32[]{:S(2)}, u32[]{:S(2)}) collective-permute-start(f32[128]{0:T(128)S(1)} %get-tuple-element.25), channel_id=1, source_target_pairs={{0,2},{2,4},{4,6},{6,8},{8,10},{10,12},{12,14},{14,16},{16,18},{18... | collective-permute-start | bytes 1544 | tf_op jit(solution)/shard_map/ppermute | solution.py:13
  150.8 6.1 %collective-permute-start.9 = (bf16[128,2048]{1,0:T(8,128)(2,1)S(1)}, bf16[128,2048]{1,0:T(8,128)(2,1)S(1)}, u32[]{:S(2)}, u32[]{:S(2)}) collective-permute-start(bf16[128,2048]{1,0:T(8,128)(2,1)S(1)} %get-tuple-element.13), channel_id=1, source_target_pairs={{0,2},{2,4},{4,6},{6,8},{8,10},{10,12},{12,14},{14,16},{16,18},{18... | collective-permute-start | bytes 1572872 | tf_op jit(solution)/shard_map/ppermute | solution.py:13
  151.1 13.3 %collective-permute-start.14 = (f32[192,3]{0,1:T(4,128)S(1)}, f32[192,3]{0,1:T(4,128)S(1)}, u32[]{:S(2)}, u32[]{:S(2)}) collective-permute-start(f32[192,3]{0,1:T(4,128)S(1)} %constant_dynamic-slice_fusion), channel_id=1, source_target_pairs={{0,1},{1,0},{2,3},{3,2},{4,5},{5,4},{6,7},{7,6},{8,9},{9,8},{10,11... | collective-permute-start | bytes 6920 | tf_op jit(solution)/shard_map/ppermute | solution.py:74
  156.4 19.8 %collective-permute-start.6 = (bf16[192,2048]{1,0:T(8,128)(2,1)S(1)}, bf16[192,2048]{1,0:T(8,128)(2,1)S(1)}, u32[]{:S(2)}, u32[]{:S(2)}) collective-permute-start(bf16[192,2048]{1,0:T(8,128)(2,1)S(1)} %dynamic-slice_convert_fusion.1), channel_id=1, source_target_pairs={{0,1},{1,0},{2,3},{3,2},{4,5},{5,4},{6,7},{7,6},{8,9},{9,8},{10,11... | collective-permute-start | bytes 2359304 | tf_op jit(solution)/shard_map/ppermute | solution.py:74
  158.2 34.9 %collective-permute-start.11 = (bf16[192,2048]{1,0:T(8,128)(2,1)S(1)}, bf16[192,2048]{1,0:T(8,128)(2,1)S(1)}, u32[]{:S(2)}, u32[]{:S(2)}) collective-permute-start(bf16[192,2048]{1,0:T(8,128)(2,1)S(1)} %dynamic-slice_convert_fusion), channel_id=1, source_target_pairs={{0,1},{1,0},{2,3},{3,2},{4,5},{5,4},{6,7},{7,6},{8,9},{9,8},{10,11... | collective-permute-start | bytes 2359304 | tf_op jit(solution)/shard_map/ppermute | solution.py:74
Sparse Core Ops, SparseCore 0:
  9.8 37.4 all-gather.3
  49.1 33.2 all-gather.5
where the time goes:
time: 201 us
  waiting for transfers between devices  102 us (51%)
  starting transfers between devices  49.6 us (25%)
  matrix products  25.4 us (13%)
  between operations  14.3 us (7%)
  blocking collectives  5.47 us (3%)
  other arithmetic  3.09 us (2%)
    ppermute x12, starting transfers between devices, shifted(): return lax.ppermute(value, axis, pairs)  41.3 us
    ppermute x3, waiting for transfers between devices, summed(): arrived = lax.ppermute(other.astype(kind), 'dp', [(0, 1), (1, 0)])  26.9 us
    ppermute x12, waiting for transfers between devices, shifted(): return lax.ppermute(value, axis, pairs)  26.9 us
    all_gather x1, waiting for transfers between devices, on_device(): group_dy = lax.all_gather(cotangent, 'dp', axis=0, tiled=True)  26.1 us
    all_gather x1, waiting for transfers between devices, on_device(): group_x = lax.all_gather(tokens, 'dp', axis=0, tiled=True)  20.7 us
    ppermute x3, starting transfers between devices, summed(): arrived = lax.ppermute(other.astype(kind), 'dp', [(0, 1), (1, 0)])  8.21 us
    all_gather x1, blocking collectives, on_device(): group_gate = lax.all_gather(gate_probs, 'dp', axis=0, tiled=True)  5.47 us
  transfers between devices with their start and end apart: 17, of which 8 were waited for; matrix products, arithmetic and copies ran while one was open for 13% of the time, Pallas kernels for 0%

commit v1 on v0

--- a/solution.py
+++ b/solution.py
@@ -17,7 +17,9 @@
     half = lax.axis_index("dp")
     own = tokens.shape[0]
     group_x = lax.all_gather(tokens, "dp", axis=0, tiled=True)
-    group_dy = lax.all_gather(cotangent, "dp", axis=0, tiled=True)
+    group_dy = jnp.concatenate(
+        lax.all_to_all(jnp.stack([cotangent] * lax.axis_size("dp")), "dp", 0, 0), axis=0
+    )
     group_gate = lax.all_gather(gate_probs, "dp", axis=0, tiled=True)
     cycle, cap = slot_rows.shape
     group = group_x.shape[0]

time: 201 us -> 192 us (0.955)
  starting transfers between devices: 49.6 us -> 39.1 us
    all_gather x1 -> x0, waiting for transfers between devices: 26.1 us -> none  [on_device(): group_dy = lax.all_gather(cotangent, 'dp', axis=0, tiled=True)]
    ppermute x12, waiting for transfers between devices: 26.9 us -> 46.9 us  [shifted(): return lax.ppermute(value, axis, pairs)]
    ppermute x12, starting transfers between devices: 41.3 us -> 31.1 us  [shifted(): return lax.ppermute(value, axis, pairs)]
    all_gather x1, waiting for transfers between devices: 20.7 us -> 27.5 us  [on_device(): group_x = lax.all_gather(tokens, 'dp', axis=0, tiled=True)]
    ppermute x3, starting transfers between devices: 8.21 us -> 3.96 us  [summed(): arrived = lax.ppermute(other.astype(kind), 'dp', [(0, 1), (1, 0)])]
    all_to_all x0 -> x1, starting transfers between devices: none -> 4.02 us  [on_device(): lax.all_to_all(jnp.stack([cotangent] * lax.axis_size('dp')), 'dp', 0, 0)]
  transfers between devices with their start and end apart: 17 -> 17, of which waited for: 8 -> 9; matrix products, arithmetic and copies ran while one was open for 13% -> 14% of each run, Pallas kernels for 0% -> 0%
where the time goes in v1:
time: 192 us
  waiting for transfers between devices  102 us (53%)
  starting transfers between devices  39.1 us (20%)
  matrix products  24.7 us (13%)
  between operations  14.3 us (7%)
  blocking collectives  5.67 us (3%)
  other arithmetic  4.37 us (2%)
  local copies, waits for them, and re-layouts  2.03 us (1%)
    ppermute x12, waiting for transfers between devices, shifted(): return lax.ppermute(value, axis, pairs)  46.9 us
    ppermute x12, starting transfers between devices, shifted(): return lax.ppermute(value, axis, pairs)  31.1 us
    all_gather x1, waiting for transfers between devices, on_device(): group_x = lax.all_gather(tokens, 'dp', axis=0, tiled=True)  27.5 us
    ppermute x3, waiting for transfers between devices, summed(): arrived = lax.ppermute(other.astype(kind), 'dp', [(0, 1), (1, 0)])  26.9 us
    all_gather x1, blocking collectives, on_device(): group_gate = lax.all_gather(gate_probs, 'dp', axis=0, tiled=True)  5.67 us
    all_to_all x1, starting transfers between devices, on_device(): lax.all_to_all(jnp.stack([cotangent] * lax.axis_size('dp')), 'dp', 0, 0)  4.02 us
    ppermute x3, starting transfers between devices, summed(): arrived = lax.ppermute(other.astype(kind), 'dp', [(0, 1), (1, 0)])  3.96 us
  transfers between devices with their start and end apart: 17, of which 9 were waited for; matrix products, arithmetic and copies ran while one was open for 14% of the time, Pallas kernels for 0%

profile of v1, /device:TPU:1, one launch (start us, length us, event | category | flops | bytes accessed | tf_op | source)
XLA Modules:
  0.0 192.1 jit_solution(3043337603893390686)
XLA Ops:
  7.2 0.7 all-gather.3.cloned.1.call-update
  7.9 5.7 %all-gather = bf16[2,192,3]{1,2,0:T(4,128)(2,1)S(1)} all-gather(bf16[1,192,3]{1,2,0:T(4,128)(2,1)} %bitcast.80), channel_id=1, replica_groups=mesh['blk'=128,'dp'=2] {'dp'}, dimensions={0}, use_global_device_ids=true | all-gather | bytes 3456 | tf_op jit(solution)/shard_map/all_gather | solution.py:23
  13.7 1.0 fusion.27
  14.7 8.9 %collective-permute-start.3 = (bf16[128]{0:T(256)(128)(2,1)S(1)}, bf16[128]{0:T(256)(128)(2,1)S(1)}, u32[]{:S(2)}, u32[]{:S(2)}) collective-permute-start(bf16[128]{0:T(256)(128)(2,1)S(1)} %get-tuple-element.29), channel_id=1, source_target_pairs={{0,252},{2,254},{4,0},{6,2},{8,4},{10,6},{12,8},{14,10},{16,12},{1... | collective-permute-start | bytes 776 | tf_op jit(solution)/shard_map/ppermute | solution.py:13
  23.6 2.1 %collective-permute-start.2 = (bf16[128]{0:T(256)(128)(2,1)S(1)}, bf16[128]{0:T(256)(128)(2,1)S(1)}, u32[]{:S(2)}, u32[]{:S(2)}) collective-permute-start(bf16[128]{0:T(256)(128)(2,1)S(1)} %get-tuple-element.30), channel_id=1, source_target_pairs={{0,254},{2,0},{4,2},{6,4},{8,6},{10,8},{12,10},{14,12},{16,14},{18... | collective-permute-start | bytes 776 | tf_op jit(solution)/shard_map/ppermute | solution.py:13
  25.7 1.3 pad_maximum_fusion.1
  26.9 4.0 %all-to-all-start = ((bf16[2,192,2048]{2,1,0:T(8,128)(2,1)}), bf16[2,192,2048]{2,1,0:T(8,128)(2,1)S(1)}, u32[]{:S(2)}, u32[]{:S(2)}) async-start(bf16[2,192,2048]{2,1,0:T(8,128)(2,1)} %pad_maximum_fusion.1), calls=%async_computation | async-start | bytes 3145728 | tf_op jit(solution)/shard_map/all_to_all | solution.py:21
  31.0 0.1 iota_compare_fusion
  31.2 27.5 %all-gather.3.cloned.1.call-done = bf16[384,2048]{1,0:T(8,128)(2,1)} async-done(((bf16[192,2048]{1,0:T(8,128)(2,1)}), bf16[384,2048]{1,0:T(8,128)(2,1)}) %all-gather.3.cloned.1.call-update) | async-done | bytes 1572880 | tf_op jit(solution)/shard_map/all_gather | solution.py:19
  58.6 2.4 %convolution_convert_fusion.5 = bf16[3,128,2048]{2,1,0:T(8,128)(2,1)S(1)} fusion(bf16[384,2048]{1,0:T(8,128)(2,1)} %all-gather.3.cloned.1.call-done, s32[3,128]{1,0:T(4,128)S(1)} %copy-done.5), kind=kOutput, calls=%fused_computation.6 | convolution fusion | flops 604913664 | bytes 3147264 | tf_op jit(solution)/shard_map/sct,td->scd/dot_general | solution.py:28
  61.1 1.2 slice_bitcast_fusion.5
  62.3 10.7 %collective-permute-start.1 = (bf16[128,2048]{1,0:T(8,128)(2,1)}, bf16[128,2048]{1,0:T(8,128)(2,1)}, u32[]{:S(2)}, u32[]{:S(2)}) collective-permute-start(bf16[128,2048]{1,0:T(8,128)(2,1)} %get-tuple-element.21), channel_id=1, source_target_pairs={{0,252},{2,254},{4,0},{6,2},{8,4},{10,6},{12,8},{14,10},{16,12},{1... | collective-permute-start | bytes 1572872 | tf_op jit(solution)/shard_map/ppermute | solution.py:13
  73.0 1.0 collective-permute-start
  74.0 1.0 convolution_convert_fusion.3
  75.1 0.3 collective-permute-start.8
  75.5 0.3 collective-permute-start.7
  75.8 8.1 %collective-permute-done.1 = bf16[128,2048]{1,0:T(8,128)(2,1)} collective-permute-done((bf16[128,2048]{1,0:T(8,128)(2,1)}, bf16[128,2048]{1,0:T(8,128)(2,1)}, u32[]{:S(2)}, u32[]{:S(2)}) %collective-permute-start.1) | collective-permute-done | bytes 524320 | tf_op jit(solution)/shard_map/ppermute | solution.py:13
  83.8 5.4 %collective-permute-done = bf16[128,2048]{1,0:T(8,128)(2,1)} collective-permute-done((bf16[128,2048]{1,0:T(8,128)(2,1)}, bf16[128,2048]{1,0:T(8,128)(2,1)}, u32[]{:S(2)}, u32[]{:S(2)}) %collective-permute-start) | collective-permute-done | bytes 524320 | tf_op jit(solution)/shard_map/ppermute | solution.py:13
  89.2 2.3 %fusion.19 = f32[384,384]{0,1:T(8,128)S(1)} fusion(bf16[1,2048,384]{2,1,0:T(8,128)(2,1)S(1)} %copy-done.2, bf16[128,2048]{1,0:T(8,128)(2,1)} %collective-permute-done.1, bf16[128,2048]{1,0:T(8,128)(2,1)} %collective-permute-done, bf16[128,2048]{1,0:T(8,128)(2,1)S(1)} %copy-done.4), kind=kOutput, calls=%fused_computation.29 | convolution fusion | flops 608698368 | bytes 3735552 | tf_op jit(solution)/shard_map/dot_general | solution.py:41
  91.6 2.2 %fusion.23 = f32[384,384]{0,1:T(8,128)S(1)} fusion(bf16[1,2048,384]{2,1,0:T(8,128)(2,1)S(1)} %copy-done.1, bf16[128,2048]{1,0:T(8,128)(2,1)} %collective-permute-done.1, bf16[128,2048]{1,0:T(8,128)(2,1)} %collective-permute-done, bf16[128,2048]{1,0:T(8,128)(2,1)S(1)} %copy-done.4), kind=kOutput, calls=%fused_computation.33 | convolution fusion | flops 608698368 | bytes 3735552 | tf_op jit(solution)/shard_map/dot_general | solution.py:40
  93.9 1.1 collective-permute-done.8
  95.0 5.4 %collective-permute-done.7 = bf16[128,2048]{1,0:T(8,128)(2,1)S(1)} collective-permute-done((bf16[128,2048]{1,0:T(8,128)(2,1)S(1)}, bf16[128,2048]{1,0:T(8,128)(2,1)S(1)}, u32[]{:S(2)}, u32[]{:S(2)}) %collective-permute-start.7) | collective-permute-done | bytes 524320 | tf_op jit(solution)/shard_map/ppermute | solution.py:13
  100.4 1.2 multiply_reduce_fusion
  101.6 1.0 convolution_convert_fusion.4
  102.7 1.6 collective-permute-start.5
  104.3 0.1 collective-permute-start.4
  104.4 1.0 fusion.21
  105.4 1.0 add_convert_fusion
  106.5 0.2 fusion.37
  106.7 1.5 collective-permute-start.10
  108.2 3.3 %collective-permute-start.13 = (f32[128]{0:T(128)S(1)}, f32[128]{0:T(128)S(1)}, u32[]{:S(2)}, u32[]{:S(2)}) collective-permute-start(f32[128]{0:T(128)S(1)} %get-tuple-element.26), channel_id=1, source_target_pairs={{0,4},{2,6},{4,8},{6,10},{8,12},{10,14},{12,16},{14,18},{16,20},{1... | collective-permute-start | bytes 1544 | tf_op jit(solution)/shard_map/ppermute | solution.py:13
  111.5 1.2 collective-permute-start.12
  112.8 3.5 %fusion = bf16[1,2048,384]{2,1,0:T(8,128)(2,1)} fusion(bf16[384,384]{0,1:T(8,128)(2,1)S(1)} %get-tuple-element.10, bf16[128,2048]{1,0:T(8,128)(2,1)} %collective-permute-done.1, bf16[128,2048]{1,0:T(8,128)(2,1)} %collective-permute-done, bf16[128,2048]{1,0:T(8,128)(2,1)S(1)} %copy-done.4), kind=kOutput, calls=%fused_computation.7 | convolution fusion | flops 609484800 | bytes 3440640 | tf_op jit(solution)/shard_map/cd,ch->dh/dot_general | solution.py:61
  116.3 3.5 %fusion.1 = bf16[1,2048,384]{2,1,0:T(8,128)(2,1)} fusion(bf16[384,384]{0,1:T(8,128)(2,1)S(1)} %get-tuple-element.24, bf16[128,2048]{1,0:T(8,128)(2,1)} %collective-permute-done.1, bf16[128,2048]{1,0:T(8,128)(2,1)} %collective-permute-done, bf16[128,2048]{1,0:T(8,128)(2,1)S(1)} %copy-done.4), kind=kOutput, calls=%fused_computation.8 | convolution fusion | flops 609484800 | bytes 3440640 | tf_op jit(solution)/shard_map/cd,ch->dh/dot_general | solution.py:62
  119.8 25.4 %collective-permute-done.13 = f32[128]{0:T(128)S(1)} collective-permute-done((f32[128]{0:T(128)S(1)}, f32[128]{0:T(128)S(1)}, u32[]{:S(2)}, u32[]{:S(2)}) %collective-permute-start.13) | collective-permute-done | bytes 544 | tf_op jit(solution)/shard_map/ppermute | solution.py:13
  145.2 0.2 select_reduce_fusion.2
  145.5 0.8 collective-permute-start.14
  146.3 1.1 fusion.3
  147.5 2.3 %collective-permute-start.6 = (bf16[192,2048]{1,0:T(8,128)(2,1)S(1)}, bf16[192,2048]{1,0:T(8,128)(2,1)S(1)}, u32[]{:S(2)}, u32[]{:S(2)}) collective-permute-start(bf16[192,2048]{1,0:T(8,128)(2,1)S(1)} %dynamic-slice_convert_fusion.1), channel_id=1, source_target_pairs={{0,1},{1,0},{2,3},{3,2},{4,5},{5,4},{6,7},{7,6},{8,9},{9,8},{10,11... | collective-permute-start | bytes 2359304 | tf_op jit(solution)/shard_map/ppermute | solution.py:76
  149.8 1.5 collective-permute-done.9
  151.3 1.1 fusion.9
  152.5 0.9 collective-permute-start.11
  153.4 2.1 %fusion.2 = bf16[1,384,2048]{2,1,0:T(8,128)(2,1)} fusion(bf16[384,384]{0,1:T(8,128)(2,1)S(1)} %get-tuple-element.23, bf16[128,2048]{1,0:T(8,128)(2,1)S(1)} %collective-permute-done.8, bf16[128,2048]{1,0:T(8,128)(2,1)S(1)} %collective-permute-done.7, bf16[128,2048]{1,0:T(8,128)(2,1)S(1)} %get-tuple-element.14), kind=kOutput, calls=%fused_computation.9 | convolution fusion | flops 609484800 | bytes 3440640 | tf_op jit(solution)/shard_map/ch,cd->hd/dot_general | solution.py:63
  155.5 0.7 dynamic-slice_add_fusion
  156.2 11.1 %collective-permute-done.6 = bf16[192,2048]{1,0:T(8,128)(2,1)S(1)} collective-permute-done((bf16[192,2048]{1,0:T(8,128)(2,1)S(1)}, bf16[192,2048]{1,0:T(8,128)(2,1)S(1)}, u32[]{:S(2)}, u32[]{:S(2)}) %collective-permute-start.6) | collective-permute-done | bytes 786464 | tf_op jit(solution)/shard_map/ppermute | solution.py:76
  167.3 1.1 add_convert_fusion.2
  168.4 15.8 %collective-permute-done.11 = bf16[192,2048]{1,0:T(8,128)(2,1)S(1)} collective-permute-done((bf16[192,2048]{1,0:T(8,128)(2,1)S(1)}, bf16[192,2048]{1,0:T(8,128)(2,1)S(1)}, u32[]{:S(2)}, u32[]{:S(2)}) %collective-permute-start.11) | collective-permute-done | bytes 786464 | tf_op jit(solution)/shard_map/ppermute | solution.py:76
  184.2 1.1 add_convert_fusion.1
  (37 shorter events, 0.8 us)
Async XLA Ops:
  7.2 93.2 %copy-start = (bf16[1,384,2048]{2,1,0:T(8,128)(2,1)S(1)}, bf16[1,384,2048]{2,1,0:T(8,128)(2,1)}, u32[]{:S(2)}) copy-start(bf16[1,384,2048]{2,1,0:T(8,128)(2,1)} %param.13) | copy-start | bytes 4718596
  7.2 18.5 %copy-start.3 = (bf16[192,2048]{1,0:T(8,128)(2,1)S(1)}, bf16[192,2048]{1,0:T(8,128)(2,1)}, u32[]{:S(2)}) copy-start(bf16[192,2048]{1,0:T(8,128)(2,1)} %param.8) | copy-start | bytes 2359300
  7.2 51.4 %all-gather.3.cloned.1.call-start = ((), (), s32[]{:S(2)}) async-start(), calls=%async_computation.1 | async-start | bytes 2359296 | tf_op jit(solution)/shard_map/all_gather | solution.py:19
  14.7 16.4 %collective-permute-start.3 = (bf16[128]{0:T(256)(128)(2,1)S(1)}, bf16[128]{0:T(256)(128)(2,1)S(1)}, u32[]{:S(2)}, u32[]{:S(2)}) collective-permute-start(bf16[128]{0:T(256)(128)(2,1)S(1)} %get-tuple-element.29), channel_id=1, source_target_pairs={{0,252},{2,254},{4,0},{6,2},{8,4},{10,6},{12,8},{14,10},{16,12},{1... | collective-permute-start | bytes 776 | tf_op jit(solution)/shard_map/ppermute | solution.py:13
  23.6 7.6 %collective-permute-start.2 = (bf16[128]{0:T(256)(128)(2,1)S(1)}, bf16[128]{0:T(256)(128)(2,1)S(1)}, u32[]{:S(2)}, u32[]{:S(2)}) collective-permute-start(bf16[128]{0:T(256)(128)(2,1)S(1)} %get-tuple-element.30), channel_id=1, source_target_pairs={{0,254},{2,0},{4,2},{6,4},{8,6},{10,8},{12,10},{14,12},{16,14},{18... | collective-permute-start | bytes 776 | tf_op jit(solution)/shard_map/ppermute | solution.py:13
  26.9 4.0 %copy-start.5 = (s32[3,128]{1,0:T(4,128)S(1)}, s32[3,128]{1,0:T(4,128)}, u32[]{:S(2)}) copy-start(s32[3,128]{1,0:T(4,128)} %param.10) | copy-start | bytes 4612
  26.9 47.0 %all-to-all-start = ((bf16[2,192,2048]{2,1,0:T(8,128)(2,1)}), bf16[2,192,2048]{2,1,0:T(8,128)(2,1)S(1)}, u32[]{:S(2)}, u32[]{:S(2)}) async-start(bf16[2,192,2048]{2,1,0:T(8,128)(2,1)} %pad_maximum_fusion.1), calls=%async_computation | async-start | bytes 3145728 | tf_op jit(solution)/shard_map/all_to_all | solution.py:21
  62.3 21.6 %collective-permute-start.1 = (bf16[128,2048]{1,0:T(8,128)(2,1)}, bf16[128,2048]{1,0:T(8,128)(2,1)}, u32[]{:S(2)}, u32[]{:S(2)}) collective-permute-start(bf16[128,2048]{1,0:T(8,128)(2,1)} %get-tuple-element.21), channel_id=1, source_target_pairs={{0,252},{2,254},{4,0},{6,2},{8,4},{10,6},{12,8},{14,10},{16,12},{1... | collective-permute-start | bytes 1572872 | tf_op jit(solution)/shard_map/ppermute | solution.py:13
  73.0 16.3 %collective-permute-start = (bf16[128,2048]{1,0:T(8,128)(2,1)}, bf16[128,2048]{1,0:T(8,128)(2,1)}, u32[]{:S(2)}, u32[]{:S(2)}) collective-permute-start(bf16[128,2048]{1,0:T(8,128)(2,1)} %get-tuple-element.22), channel_id=1, source_target_pairs={{0,254},{2,0},{4,2},{6,4},{8,6},{10,8},{12,10},{14,12},{16,14},{18... | collective-permute-start | bytes 1572872 | tf_op jit(solution)/shard_map/ppermute | solution.py:13
  75.0 14.2 %copy-start.2 = (bf16[1,2048,384]{2,1,0:T(8,128)(2,1)S(1)}, bf16[1,2048,384]{2,1,0:T(8,128)(2,1)}, u32[]{:S(2)}) copy-start(bf16[1,2048,384]{2,1,0:T(8,128)(2,1)} %param.12) | copy-start | bytes 4718596
  75.0 14.2 %copy-start.4 = (bf16[128,2048]{1,0:T(8,128)(2,1)S(1)}, bf16[128,2048]{1,0:T(8,128)(2,1)}, u32[]{:S(2)}) copy-start(bf16[128,2048]{1,0:T(8,128)(2,1)} %get-tuple-element.20) | copy-start | bytes 1572868
  75.1 19.8 %collective-permute-start.8 = (bf16[128,2048]{1,0:T(8,128)(2,1)S(1)}, bf16[128,2048]{1,0:T(8,128)(2,1)S(1)}, u32[]{:S(2)}, u32[]{:S(2)}) collective-permute-start(bf16[128,2048]{1,0:T(8,128)(2,1)S(1)} %get-tuple-element.15), channel_id=1, source_target_pairs={{0,252},{2,254},{4,0},{6,2},{8,4},{10,6},{12,8},{14,10},{16,12},{1... | collective-permute-start | bytes 1572872 | tf_op jit(solution)/shard_map/ppermute | solution.py:13
  75.5 24.9 %collective-permute-start.7 = (bf16[128,2048]{1,0:T(8,128)(2,1)S(1)}, bf16[128,2048]{1,0:T(8,128)(2,1)S(1)}, u32[]{:S(2)}, u32[]{:S(2)}) collective-permute-start(bf16[128,2048]{1,0:T(8,128)(2,1)S(1)} %get-tuple-element.16), channel_id=1, source_target_pairs={{0,254},{2,0},{4,2},{6,4},{8,6},{10,8},{12,10},{14,12},{16,14},{18... | collective-permute-start | bytes 1572872 | tf_op jit(solution)/shard_map/ppermute | solution.py:13
  89.2 2.4 %copy-start.1 = (bf16[1,2048,384]{2,1,0:T(8,128)(2,1)S(1)}, bf16[1,2048,384]{2,1,0:T(8,128)(2,1)}, u32[]{:S(2)}) copy-start(bf16[1,2048,384]{2,1,0:T(8,128)(2,1)} %param.11) | copy-start | bytes 4718596
  102.7 43.6 %collective-permute-start.5 = (bf16[128,2048]{1,0:T(8,128)(2,1)S(1)}, bf16[128,2048]{1,0:T(8,128)(2,1)S(1)}, u32[]{:S(2)}, u32[]{:S(2)}) collective-permute-start(bf16[128,2048]{1,0:T(8,128)(2,1)S(1)} %get-tuple-element.18), channel_id=1, source_target_pairs={{0,4},{2,6},{4,8},{6,10},{8,12},{10,14},{12,16},{14,18},{16,20},{1... | collective-permute-start | bytes 1572872 | tf_op jit(solution)/shard_map/ppermute | solution.py:13
  104.3 42.0 %collective-permute-start.4 = (bf16[128,2048]{1,0:T(8,128)(2,1)S(1)}, bf16[128,2048]{1,0:T(8,128)(2,1)S(1)}, u32[]{:S(2)}, u32[]{:S(2)}) collective-permute-start(bf16[128,2048]{1,0:T(8,128)(2,1)S(1)} %get-tuple-element.19), channel_id=1, source_target_pairs={{0,2},{2,4},{4,6},{6,8},{8,10},{10,12},{12,14},{14,16},{16,18},{18... | collective-permute-start | bytes 1572872 | tf_op jit(solution)/shard_map/ppermute | solution.py:13
  106.7 43.1 %collective-permute-start.10 = (bf16[128,2048]{1,0:T(8,128)(2,1)S(1)}, bf16[128,2048]{1,0:T(8,128)(2,1)S(1)}, u32[]{:S(2)}, u32[]{:S(2)}) collective-permute-start(bf16[128,2048]{1,0:T(8,128)(2,1)S(1)} %get-tuple-element.12), channel_id=1, source_target_pairs={{0,4},{2,6},{4,8},{6,10},{8,12},{10,14},{12,16},{14,18},{16,20},{1... | collective-permute-start | bytes 1572872 | tf_op jit(solution)/shard_map/ppermute | solution.py:13
  108.2 37.0 %collective-permute-start.13 = (f32[128]{0:T(128)S(1)}, f32[128]{0:T(128)S(1)}, u32[]{:S(2)}, u32[]{:S(2)}) collective-permute-start(f32[128]{0:T(128)S(1)} %get-tuple-element.26), channel_id=1, source_target_pairs={{0,4},{2,6},{4,8},{6,10},{8,12},{10,14},{12,16},{14,18},{16,20},{1... | collective-permute-start | bytes 1544 | tf_op jit(solution)/shard_map/ppermute | solution.py:13
  111.5 33.6 %collective-permute-start.12 = (f32[128]{0:T(128)S(1)}, f32[128]{0:T(128)S(1)}, u32[]{:S(2)}, u32[]{:S(2)}) collective-permute-start(f32[128]{0:T(128)S(1)} %get-tuple-element.25), channel_id=1, source_target_pairs={{0,2},{2,4},{4,6},{6,8},{8,10},{10,12},{12,14},{14,16},{16,18},{18... | collective-permute-start | bytes 1544 | tf_op jit(solution)/shard_map/ppermute | solution.py:13
  145.2 6.1 %collective-permute-start.9 = (bf16[128,2048]{1,0:T(8,128)(2,1)S(1)}, bf16[128,2048]{1,0:T(8,128)(2,1)S(1)}, u32[]{:S(2)}, u32[]{:S(2)}) collective-permute-start(bf16[128,2048]{1,0:T(8,128)(2,1)S(1)} %get-tuple-element.13), channel_id=1, source_target_pairs={{0,2},{2,4},{4,6},{6,8},{8,10},{10,12},{12,14},{14,16},{16,18},{18... | collective-permute-start | bytes 1572872 | tf_op jit(solution)/shard_map/ppermute | solution.py:13
  145.5 10.1 %collective-permute-start.14 = (f32[192,3]{0,1:T(4,128)S(1)}, f32[192,3]{0,1:T(4,128)S(1)}, u32[]{:S(2)}, u32[]{:S(2)}) collective-permute-start(f32[192,3]{0,1:T(4,128)S(1)} %constant_dynamic-slice_fusion), channel_id=1, source_target_pairs={{0,1},{1,0},{2,3},{3,2},{4,5},{5,4},{6,7},{7,6},{8,9},{9,8},{10,11... | collective-permute-start | bytes 6920 | tf_op jit(solution)/shard_map/ppermute | solution.py:76
  147.5 19.8 %collective-permute-start.6 = (bf16[192,2048]{1,0:T(8,128)(2,1)S(1)}, bf16[192,2048]{1,0:T(8,128)(2,1)S(1)}, u32[]{:S(2)}, u32[]{:S(2)}) collective-permute-start(bf16[192,2048]{1,0:T(8,128)(2,1)S(1)} %dynamic-slice_convert_fusion.1), channel_id=1, source_target_pairs={{0,1},{1,0},{2,3},{3,2},{4,5},{5,4},{6,7},{7,6},{8,9},{9,8},{10,11... | collective-permute-start | bytes 2359304 | tf_op jit(solution)/shard_map/ppermute | solution.py:76
  152.5 31.7 %collective-permute-start.11 = (bf16[192,2048]{1,0:T(8,128)(2,1)S(1)}, bf16[192,2048]{1,0:T(8,128)(2,1)S(1)}, u32[]{:S(2)}, u32[]{:S(2)}) collective-permute-start(bf16[192,2048]{1,0:T(8,128)(2,1)S(1)} %dynamic-slice_convert_fusion), channel_id=1, source_target_pairs={{0,1},{1,0},{2,3},{3,2},{4,5},{5,4},{6,7},{7,6},{8,9},{9,8},{10,11... | collective-permute-start | bytes 2359304 | tf_op jit(solution)/shard_map/ppermute | solution.py:76
Sparse Core Ops, SparseCore 0:
  9.8 48.7 all-gather.2
